TPU v7x, 32 devices: a whole 2x2x4 slice. The times are simulated.
32 devices in a mesh: rep: 2 (over y), cp: 4 (over z), tp: 4 (over x, core).
Axes of the slice: x: 2, y: 2, z: 4, core: 2. Of those that a mesh axis runs over, the one named last changes fastest.
Arguments:
- queries: bfloat16 [2048, 8192], P(('rep', 'cp'), 'tp'), parts along dimension 0, may hold values from -16 to 16
- keys: bfloat16 [2048, 1024], P(('rep', 'cp'), 'tp'), parts along dimension 0, may hold values from -16 to 16
- values: bfloat16 [2048, 1024], P(('rep', 'cp'), 'tp'), parts along dimension 0, may hold values from -6 to 6
- segment_ids: int32 [2048], P(('rep', 'cp')), parts along dimension 0, may hold values from 0 to 3, never falling along the last dimension, each value on 1 to 768 neighbouring positions
Outputs:
- attended: bfloat16 [2048, 8192], P(('rep', 'cp'), 'tp'), parts along dimension 0
There are 2 independent parts, one for each index of `rep`. A program takes and returns all parts, laid end to end along the dimension named above; each array names one. Nothing has to cross between parts.
Inputs may be any that keep to these rules, and one draw needn't show every extreme that they name: `segment_ids`: segment ids never fall along the sequence of one part.
All inputs are finite; a program needn't handle non-finite values.
Results may differ from a plain program's by a relative error of at most 0.012.
Values may be sent and summed in bfloat16 or wider, within the bound.
A program may use at most 64 MiB of HBM per device.

v0:
```python
import math

import jax
import jax.numpy as jnp
from jax import lax
from jax.sharding import PartitionSpec as P

HEAD_DIM = 128


rope_base = 500000.0


def rotate(vectors, positions):
    half = vectors.shape[-1] // 2
    freq = rope_base ** (-jnp.arange(half, dtype=jnp.float32) * 2.0 / vectors.shape[-1])
    angle = positions.astype(jnp.float32)[:, None] * freq[None, :]
    cosine = jnp.cos(angle)[:, None, :]
    sine = jnp.sin(angle)[:, None, :]
    first = vectors[..., :half]
    second = vectors[..., half:]
    return jnp.concatenate(
        [first * cosine - second * sine, second * cosine + first * sine], axis=-1
    )


def body(queries, keys, values, segment_ids):
    tok_rows = queries.shape[0]
    half_rows = tok_rows // 2
    cycle_place = lax.axis_index("cp")
    offset = cycle_place * tok_rows
    local_index = offset + jnp.arange(tok_rows, dtype=jnp.int32)
    every_id = lax.all_gather(segment_ids, "cp", axis=0, tiled=True)
    starts = jnp.sum((every_id[None, :] < segment_ids[:, None]).astype(jnp.int32), axis=1)
    positions = local_index - starts
    heads_local = queries.shape[1] // HEAD_DIM
    kv_local = keys.shape[1] // HEAD_DIM
    group = heads_local // kv_local
    rot_q = rotate(
        queries.astype(jnp.float32).reshape(tok_rows, heads_local, HEAD_DIM), positions
    ).astype(jnp.bfloat16)
    rot_k = rotate(
        keys.astype(jnp.float32).reshape(tok_rows, kv_local, HEAD_DIM), positions
    ).astype(jnp.bfloat16)
    rot_q = rot_q.reshape(tok_rows, heads_local * HEAD_DIM)
    rot_k = rot_k.reshape(tok_rows, kv_local * HEAD_DIM)
    lower_rows = rot_q[:half_rows]
    upper_rows = rot_q[half_rows:]
    lower_starts = starts[:half_rows]
    upper_starts = starts[half_rows:]
    lower_index = local_index[:half_rows]
    upper_index = local_index[half_rows:]
    query_heads = jnp.concatenate([lower_rows, upper_rows], axis=0).reshape(
        tok_rows, kv_local, group, HEAD_DIM
    )
    query_index = jnp.concatenate([lower_index, upper_index], axis=0)
    query_starts = jnp.concatenate([lower_starts, upper_starts], axis=0)
    lowest_start = jnp.min(query_starts)
    highest_row = jnp.max(query_index)
    scale = 1.0 / math.sqrt(HEAD_DIM)
    fresh = (
        jnp.full((kv_local, group, tok_rows), -1e30, jnp.float32),
        jnp.zeros((kv_local, group, tok_rows), jnp.float32),
        jnp.zeros((tok_rows, kv_local, group, HEAD_DIM), jnp.float32),
    )
    key_piece = lax.all_gather(rot_k, "cp", axis=0, tiled=True)
    value_piece = lax.all_gather(values, "cp", axis=0, tiled=True)
    length = key_piece.shape[0]
    key_block = math.gcd(length, 1024)
    blocks = length // key_block
    key_parts = key_piece.reshape(blocks, key_block, kv_local, HEAD_DIM)
    value_parts = value_piece.reshape(blocks, key_block, kv_local, HEAD_DIM)

    def step(state, packed):
        key_part, value_part, number = packed
        column_index = number * key_block + jnp.arange(key_block, dtype=jnp.int32)
        keep = (column_index[None, :] <= query_index[:, None]) & (
            column_index[None, :] >= query_starts[:, None]
        )

        def update(inner):
            running_top, running_total, summed = inner
            scores = (
                jnp.einsum(
                    "tgjd,kgd->gjtk", query_heads, key_part, preferred_element_type=jnp.float32
                )
                * scale
            )
            scores = jnp.where(keep[None, None], scores, -1e30)
            new_top = jnp.maximum(running_top, jnp.max(scores, axis=-1))
            weights = jnp.where(keep[None, None], jnp.exp(scores - new_top[..., None]), 0.0)
            factor = jnp.exp(running_top - new_top)
            new_total = running_total * factor + jnp.sum(weights, axis=-1)
            product = jnp.einsum(
                "gjtk,kgd->tgjd",
                weights.astype(jnp.bfloat16),
                value_part,
                preferred_element_type=jnp.float32,
            )
            new_summed = summed * jnp.transpose(factor, (2, 0, 1))[..., None] + product
            return (new_top, new_total, new_summed)

        visible = (column_index[0] <= highest_row) & (column_index[-1] >= lowest_start)
        return (lax.cond(visible, update, lambda inner: inner, state), None)

    result, unused = lax.scan(
        step, fresh, (key_parts, value_parts, jnp.arange(blocks, dtype=jnp.int32))
    )
    running_top, running_total, summed = result
    result = (summed / jnp.transpose(running_total, (2, 0, 1))[..., None]).astype(jnp.bfloat16)
    result = result.reshape(tok_rows, heads_local * HEAD_DIM)
    lower_out = result[:half_rows]
    upper_out = result[half_rows:]
    return jnp.concatenate([lower_out, upper_out], axis=0)


def solution(mesh):
    return jax.shard_map(
        body,
        mesh=mesh,
        in_specs=(
            P(("rep", "cp"), "tp"),
            P(("rep", "cp"), "tp"),
            P(("rep", "cp"), "tp"),
            P(("rep", "cp")),
        ),
        out_specs=P(("rep", "cp"), "tp"),
        check_vma=False,
    )
```

profile of v0, /device:TPU:0, one launch (start us, length us, event | category | flops | bytes accessed | tf_op | source)
XLA Modules:
  0.0 77.3 jit_solution(5024197564219296240)
XLA Ops:
  0.0 13.0 %all-gather = s32[4,1,256]{2,1,0:T(1,128)S(1)} all-gather(s32[1,1,256]{2,1,0:T(1,128)} %bitcast.59), channel_id=1, replica_groups=mesh['rep'=2,'cp'=4,'tp'=4] {'cp'}, dimensions={0}, use_global_device_ids=true | all-gather | bytes 5120 | tf_op jit(solution)/shard_map/all_gather | solution.py:33
  13.0 0.9 %convert_reduce_fusion = s32[256]{0:T(256)S(1)} fusion(s32[1024]{0:T(1024)S(1)} %bitcast.57, s32[256]{0:T(256)} %param.9), kind=kLoop, calls=%fused_computation.28 | loop fusion | flops 786176 | bytes 6144 | tf_op jit(solution)/shard_map/reduce_sum | solution.py:34
  14.0 0.7 subtract_convert_fusion.2
  14.7 0.6 fusion.19
  17.8 0.5 multiply_cosine_fusion
  18.3 1.0 %reshape.105 = f32[256,2,128]{2,1,0:T(2,128)S(1)} reshape(bf16[256,256]{1,0:T(8,128)(2,1)} %param.7) | data formatting | bytes 393216 | tf_op jit(solution)/shard_map/reshape | solution.py:43
  19.3 0.5 subtract_convert_fusion.1
  19.8 0.4 pad_maximum_fusion.3
  20.2 15.5 %all_gather.10 = bf16[1024,256]{1,0:T(8,128)(2,1)} all-gather(bf16[256,256]{1,0:T(8,128)(2,1)S(1)} %bitcast.54), channel_id=1, replica_groups=mesh['rep'=2,'cp'=4,'tp'=4] {'cp'}, dimensions={0}, use_global_device_ids=true | all-gather | bytes 655360 | tf_op jit(solution)/shard_map/all_gather | solution.py:66
  35.8 15.8 %all_gather.11 = bf16[1024,256]{1,0:T(8,128)(2,1)} all-gather(bf16[256,256]{1,0:T(8,128)(2,1)S(1)} %copy-done.3), channel_id=1, replica_groups=mesh['rep'=2,'cp'=4,'tp'=4] {'cp'}, dimensions={0}, use_global_device_ids=true | all-gather | bytes 655360 | tf_op jit(solution)/shard_map/all_gather | solution.py:67
  52.1 0.4 copy.36
  52.5 0.7 fusion.17
  53.2 1.4 %subtract_convert_fusion = (bf16[256,16,64]{2,0,1:T(8,128)(2,1)S(1)}, bf16[256,16,64]{2,0,1:T(8,128)(2,1)S(1)}) fusion(f32[256,16,64]{2,1,0:T(8,128)S(1)} %get-tuple-element.131, f32[256,16,64]{2,1,0:T(8,128)S(1)} %get-tuple-element.130, f32[256,64]{1,0:T(8,128)S(1)} %get-tuple-element.139, f32[256,64]{1,0:T(8,128)S(1)} %get-tuple-element.138), kind=kLoop, calls=%fused_computation.23 | loop fusion | flops 2097152 | bytes 3276800 | tf_op jit(solution)/shard_map/convert.2
  54.5 0.6 fusion.15
  55.1 1.1 %pad_maximum_fusion = bf16[256,2,8,128]{3,0,2,1:T(8,128)(2,1)} fusion(bf16[128,2,8,128]{3,0,2,1:T(8,128)(2,1)S(1)} %bitcast.52, bf16[128,2,8,128]{3,0,2,1:T(8,128)(2,1)S(1)} %bitcast.51), kind=kLoop, calls=%fused_computation.26 | loop fusion | flops 2097152 | bytes 2097152 | tf_op jit(solution)/shard_map/concatenate | solution.py:53
  56.2 18.2 %conditional.1 = ((f32[2,8,256]{2,1,0:T(8,128)S(1)}, f32[256,2,8,128]{3,0,2,1:T(8,128)S(1)})) conditional(s32[]{:T(128)} %convert_element_type.32, (f32[2,8,256]{2,1,0:T(8,128)S(1)}, f32[256,2,8,128]{3,0,2,1:T(8,128)S(1)}) %tuple.25, (s32[]{:T(128)}, s32[256,1]{0,1:T(1,128)S(1)}, s32[256,1024]{0,1:T(8,128)S(1)}, s32[256]{0:T(256)S(1)}, ...), branch_computations={%region_3.4_spmd, %region_4.7_spmd} | conditional | flops 2203857152 | bytes 68358232 | solution.py:104
  56.4 2.1 %squeeze.20 = bf16[1024,2,128]{2,1,0:T(2,128)(2,1)} reshape(bf16[1024,256]{1,0:T(8,128)(2,1)} %get-tuple-element.114) | data formatting | bytes 1048576 | tf_op jit(solution)/shard_map/while/body/jit(dynamic_index_in_dim)/squeeze | solution.py:106
  58.5 2.0 %squeeze.21 = bf16[1024,2,128]{2,1,0:T(2,128)(2,1)} reshape(bf16[1024,256]{1,0:T(8,128)(2,1)} %get-tuple-element.117) | data formatting | bytes 1048576 | tf_op jit(solution)/shard_map/while/body/jit(dynamic_index_in_dim)/squeeze | solution.py:106
  60.4 3.8 %fusion = (f32[2,8,256]{2,1,0:T(8,128)S(1)}, f32[2,1024,256,8]{2,1,3,0:T(8,128)S(1)}) fusion(pred[256,1024]{0,1:T(8,128)(4,1)S(1)} %compare_and_fusion, bf16[256,2,8,128]{3,0,2,1:T(8,128)(2,1)S(1)} %copy-done, bf16[1024,2,128,1]{2,1,0,3:T(2,128)(2,1)} %bitcast.46), kind=kOutput, calls=%fused_computation.2 | convolution fusion | flops 1086320640 | bytes 18628608 | tf_op jit(solution)/shard_map/while/body/eval_jaxpr/cond/branch_1_fun/tgjd,kgd->gjtk/dot_general | solution.py:84
  64.3 4.0 %fusion.2 = f32[2,8,256]{2,1,0:T(8,128)S(1)} fusion(f32[2,1024,256,8]{2,1,3,0:T(8,128)S(1)} %get-tuple-element.125, f32[2,8,256]{2,1,0:T(8,128)S(1)} %broadcast_maximum_fusion, pred[256,1024]{0,1:T(8,128)(4,1)S(1)} %compare_and_fusion), kind=kLoop, calls=%fused_computation.4 | loop fusion | flops 20967424 | bytes 17072128 | tf_op jit(solution)/shard_map/while/body/eval_jaxpr/cond/branch_1_fun/reduce_sum | solution.py:93
  68.3 6.0 %bitcast_add_fusion = f32[256,2,8,128]{3,0,2,1:T(8,128)S(1)} fusion(f32[256,2,8,128]{3,0,2,1:T(8,128)S(1)} %get-tuple-element.116, f32[2,1024,256,8]{2,1,3,0:T(8,128)S(1)} %get-tuple-element.125, f32[2,8,256]{2,1,0:T(8,128)S(1)} %broadcast_maximum_fusion, pred[256,1024]{0,1:T(8,128)(4,1)S(1)} %compare_and_fusion, f32[256,2,8]{0,2,1:T(8,128)S(1)} %get-tuple-element.122, ...), kind=kOutput, calls=%fused_computation.7 | convolution fusion | flops 1095761920 | bytes 21790720 | tf_op jit(solution)/shard_map/while/body/eval_jaxpr/cond/branch_1_fun/gjtk,kgd->tgjd/dot_general | solution.py:94
  74.3 0.7 divide_convert_fusion
  75.2 0.3 copy.24
  76.2 1.1 %pad_maximum_fusion.1 = bf16[256,2048]{1,0:T(8,128)(2,1)} fusion(bf16[128,2048]{1,0:T(8,128)(2,1)S(1)} %bitcast.50, bf16[128,2048]{1,0:T(8,128)(2,1)S(1)} %bitcast.49), kind=kLoop, calls=%fused_computation.27 | loop fusion | flops 2097152 | bytes 2097152 | tf_op jit(solution)/shard_map/concatenate | solution.py:114
  (24 shorter events, 1.5 us)
Async XLA Ops:
  0.0 35.8 %copy-start.3 = (bf16[256,256]{1,0:T(8,128)(2,1)S(1)}, bf16[256,256]{1,0:T(8,128)(2,1)}, u32[]{:S(2)}) copy-start(bf16[256,256]{1,0:T(8,128)(2,1)} %param.8) | copy-start | bytes 393220
  20.2 31.6 %copy-start.1 = (bf16[256,2048]{1,0:T(8,128)(2,1)S(1)}, bf16[256,2048]{1,0:T(8,128)(2,1)}, u32[]{:S(2)}) copy-start(bf16[256,2048]{1,0:T(8,128)(2,1)} %param.6) | copy-start | bytes 3145732
  56.4 4.0 %copy-start = (bf16[256,2,8,128]{3,0,2,1:T(8,128)(2,1)S(1)}, bf16[256,2,8,128]{3,0,2,1:T(8,128)(2,1)}, u32[]{:S(2)}) copy-start(bf16[256,2,8,128]{3,0,2,1:T(8,128)(2,1)} %get-tuple-element.115) | copy-start | bytes 3145732 | tf_op jit(solution)/shard_map/while/body/eval_jaxpr/cond
  64.2 4.0 %copy-start.2 = (bf16[1024,2,128]{2,1,0:T(2,128)(2,1)S(1)}, bf16[1024,2,128]{2,1,0:T(2,128)(2,1)}, u32[]{:S(2)}) copy-start(bf16[1024,2,128]{2,1,0:T(2,128)(2,1)} %squeeze.21) | copy-start | bytes 1572868 | tf_op jit(solution)/shard_map/while/body/eval_jaxpr/cond
where the time goes:
time: 77.6 us; the launch traced here: 77.3 us
  blocking collectives  44.3 us (57%)
  other arithmetic  12.3 us (16%)
  matrix products  9.83 us (13%)
  local copies, waits for them, and re-layouts  8.08 us (10%)
  between operations  2.69 us (3%)
    all_gather x1, blocking collectives, body(): value_piece = lax.all_gather(values, 'cp', axis=0, tiled=True)  15.8 us
    all_gather x1, blocking collectives, body(): key_piece = lax.all_gather(rot_k, 'cp', axis=0, tiled=True)  15.5 us
    all_gather x1, blocking collectives, body(): every_id = lax.all_gather(segment_ids, 'cp', axis=0, tiled=True)  13 us
    dot_general x1, matrix products, update(): jnp.einsum('gjtk,kgd->tgjd', weights.astype(jnp.bfloat16), value_part, pr...  6.05 us
    squeeze x2, local copies, waits for them, and re-layouts, body(): lax.scan(step, fresh, (key_parts, value_parts, jnp.arange(blocks, dtype=j...  4.02 us
    reduce_sum x1, other arithmetic, update(): new_total = running_total * factor + jnp.sum(weights, axis=-1)  4 us
    dot_general x1, matrix products, update(): jnp.einsum('tgjd,kgd->gjtk', query_heads, key_part, preferred_element_typ...  3.79 us
    another operation x2, other arithmetic  1.83 us

commit v1 on v0

v1 whole, which is shorter than its diff:
```python
import functools
import math

import jax
import jax.numpy as jnp
import numpy as np
from jax import lax
from jax.experimental import pallas as pl
from jax.experimental.pallas import tpu as pltpu
from jax.sharding import PartitionSpec as P

HEAD_DIM = 128
ROPE_BASE = 500000.0
HIDDEN = -1e30
MESH = pl.DeviceIdType.MESH


def tables(rows, blocks):
    half = HEAD_DIM // 2
    freq = ROPE_BASE ** (-np.arange(half, dtype=np.float64) * 2.0 / HEAD_DIM)
    sign = np.concatenate([-np.ones(half), np.ones(half)])

    def pair(positions):
        angle = np.tile(positions[:, None] * freq[None, :], (1, 2))
        return np.cos(angle), np.sin(angle) * sign

    local = np.stack(pair(np.arange(rows, dtype=np.float64)))
    base = np.stack(pair(np.arange(blocks, dtype=np.float64) * rows), axis=1)
    return local.astype(np.float32), base.astype(np.float32)


def attend(
    n, chunks, q_hbm, k_hbm, v_hbm, id_hbm, local_hbm, base_ref, out_ref,
    q_raw, q_turned, k_buf, v_buf, id_buf, local, bias, acc, top, total,
    q_sem, own_sem, send_sem, recv_sem,
):
    me = lax.axis_index("cp")
    rows = q_hbm.shape[0]
    heads = q_hbm.shape[1] // HEAD_DIM
    kv_heads = k_hbm.shape[1] // HEAD_DIM
    group = heads // kv_heads
    chunk = rows // chunks
    right = jnp.minimum(me + 1, n - 1)
    left = jnp.maximum(me - 1, 0)

    barrier = pltpu.get_barrier_semaphore()

    @pl.when(me > 0)
    def _():
        pl.semaphore_signal(barrier, inc=1, device_id={"cp": left}, device_id_type=MESH)

    def pieces(slot):
        out = [(None, id_buf.at[slot])]
        for c in range(chunks):
            part = pl.ds(c * chunk, chunk)
            out.append((k_hbm.at[part, :], k_buf.at[slot, part, :]))
            out.append((v_hbm.at[part, :], v_buf.at[slot, part, :]))
        return out

    def of_chunk(c):
        return ([0] if c == 0 else []) + [1 + 2 * c, 2 + 2 * c]

    def own_copies():
        source = [id_hbm] + [s for s, _ in pieces(0)[1:]]
        return [
            pltpu.make_async_copy(source[p], pieces(0)[p][1], own_sem.at[p])
            for p in range(1 + 2 * chunks)
        ]

    def remote(p, slot, source):
        return pltpu.make_async_remote_copy(
            src_ref=source,
            dst_ref=pieces(slot)[p][1],
            send_sem=send_sem.at[slot - 1, p],
            recv_sem=recv_sem.at[slot - 1, p],
            device_id={"cp": right},
            device_id_type=MESH,
        )

    def own_remote(p):
        return remote(p, 1, id_hbm if p == 0 else pieces(0)[p][0])

    q_copies = [pltpu.make_async_copy(q_hbm, q_raw, q_sem.at[0]),
                pltpu.make_async_copy(local_hbm, local, q_sem.at[1])]
    for copy in own_copies() + q_copies:
        copy.start()

    @pl.when(me < n - 1)
    def _():
        pl.semaphore_wait(barrier, 1)
        for p in range(1 + 2 * chunks):
            own_remote(p).start()

    def phases(block, start, size):
        row = base_ref[block]
        cb, sb = row[0:1, :], row[1:2, :]
        cr = local[0, pl.ds(start, size), :]
        sr = local[1, pl.ds(start, size), :]
        return cb * cr - sb * sr, sb * cr + cb * sr

    def turn(x, cosine, sine):
        x = x.astype(jnp.float32)
        return x * cosine + pltpu.roll(x, HEAD_DIM // 2, axis=1) * sine

    for copy in q_copies:
        copy.wait()
    cosine, sine = phases(me, 0, rows)
    scale = math.log2(math.e) / math.sqrt(HEAD_DIM)
    cosine, sine = cosine * scale, sine * scale
    for h in range(heads):
        x = turn(q_raw[:, h * HEAD_DIM:(h + 1) * HEAD_DIM], cosine, sine)
        q_turned[h] = x.T.astype(jnp.bfloat16)
    acc[...] = jnp.zeros_like(acc)
    total[...] = jnp.zeros_like(total)
    top[...] = jnp.full_like(top, HIDDEN)
    for copy in own_copies():
        copy.wait()

    row_index = lax.broadcasted_iota(jnp.int32, (chunk, rows), 1)
    key_index = lax.broadcasted_iota(jnp.int32, (chunk, rows), 0)

    def step(k, unused):
        block = me - k
        for c in range(chunks):
            @pl.when(k > 0)
            def _():
                for p in of_chunk(c):
                    remote(p, k, pieces(k)[p][1]).wait_recv()

            @pl.when((k > 0) & (me < n - 1))
            def _():
                for p in of_chunk(c):
                    remote(p, k + 1, pieces(k)[p][1]).start()

            part = pl.ds(c * chunk, chunk)
            row_id = id_buf[0].astype(jnp.float32)
            key_id = id_buf[k, :, part].astype(jnp.float32)
            key_id = jnp.broadcast_to(key_id, (HEAD_DIM, chunk)).T[:, :1]
            keep = (key_id == row_id) & (key_index + (c * chunk - k * rows) <= row_index)
            bias[...] = jnp.where(keep, 0.0, HIDDEN)
            cosine, sine = phases(block, c * chunk, chunk)
            for g in range(kv_heads):
                lanes = slice(g * HEAD_DIM, (g + 1) * HEAD_DIM)
                key = turn(k_buf[k, part, lanes], cosine, sine).astype(jnp.bfloat16)
                value = v_buf[k, part, lanes].T
                for h in range(g * group, (g + 1) * group):
                    scores = jnp.dot(key, q_turned[h], preferred_element_type=jnp.float32)
                    scores = scores + bias[...]
                    old = top[h:h + 1, :]
                    new = jnp.maximum(old, jnp.max(scores, axis=0, keepdims=True))
                    weights = jnp.exp2(scores - new)
                    factor = jnp.exp2(old - new)
                    top[h:h + 1, :] = new
                    total[h:h + 1, :] = total[h:h + 1, :] * factor + jnp.sum(
                        weights, axis=0, keepdims=True
                    )
                    acc[h] = acc[h] * factor + jnp.dot(
                        value, weights.astype(jnp.bfloat16), preferred_element_type=jnp.float32
                    )
        return unused

    lax.fori_loop(0, me + 1, step, 0)

    for h in range(heads):
        result = acc[h] * (1.0 / total[h:h + 1, :])
        out_ref[:, h * HEAD_DIM:(h + 1) * HEAD_DIM] = result.T.astype(out_ref.dtype)

    @pl.when(me < n - 1)
    def _():
        for p in range(1 + 2 * chunks):
            own_remote(p).wait_send()

        def drain(k, unused):
            for p in range(1 + 2 * chunks):
                remote(p, k + 1, pieces(k)[p][1]).wait_send()
            return unused

        lax.fori_loop(1, me + 1, drain, 0)


def body(n, queries, keys, values, segment_ids):
    rows, width = queries.shape
    kv_width = keys.shape[1]
    heads = width // HEAD_DIM
    chunks = 2
    chunk = rows // chunks
    local, base = tables(rows, n)
    anywhere = pl.BlockSpec(memory_space=pl.ANY)
    vmem = pl.BlockSpec(memory_space=pltpu.VMEM)
    count = 1 + 2 * chunks
    return pl.pallas_call(
        functools.partial(attend, n, chunks),
        out_shape=jax.ShapeDtypeStruct((rows, width), queries.dtype),
        in_specs=[anywhere] * 5 + [vmem],
        out_specs=vmem,
        scratch_shapes=[
            pltpu.VMEM((rows, width), queries.dtype),
            pltpu.VMEM((heads, HEAD_DIM, rows), jnp.bfloat16),
            pltpu.VMEM((n, rows, kv_width), keys.dtype),
            pltpu.VMEM((n, rows, kv_width), values.dtype),
            pltpu.VMEM((n, 1, rows), jnp.int32),
            pltpu.VMEM((2, rows, HEAD_DIM), jnp.float32),
            pltpu.VMEM((chunk, rows), jnp.float32),
            pltpu.VMEM((heads, HEAD_DIM, rows), jnp.float32),
            pltpu.VMEM((heads, rows), jnp.float32),
            pltpu.VMEM((heads, rows), jnp.float32),
            pltpu.SemaphoreType.DMA((2,)),
            pltpu.SemaphoreType.DMA((count,)),
            pltpu.SemaphoreType.DMA((max(n - 1, 1), count)),
            pltpu.SemaphoreType.DMA((max(n - 1, 1), count)),
        ],
        compiler_params=pltpu.CompilerParams(collective_id=0, has_side_effects=True),
    )(queries, keys, values, segment_ids.reshape(1, rows), jnp.asarray(local), jnp.asarray(base))


def solution(mesh):
    return jax.shard_map(
        functools.partial(body, mesh.shape["cp"]),
        mesh=mesh,
        in_specs=(
            P(("rep", "cp"), "tp"),
            P(("rep", "cp"), "tp"),
            P(("rep", "cp"), "tp"),
            P(("rep", "cp")),
        ),
        out_specs=P(("rep", "cp"), "tp"),
        check_vma=False,
    )
```

time: 77.6 us -> 25.4 us (0.33)
  the two profiles are of different devices: /device:TPU:0 before, /device:TPU:24 now
where the time goes in v1:
time: 25.4 us; the launch traced here: 25.2 us
  Pallas kernels  22.9 us (90%)
  local copies, waits for them, and re-layouts  2.3 us (9%)
    pallas_call x1, Pallas kernels, body(): pl.pallas_call(functools.partial(attend, n, chunks), out_shape=jax.ShapeD...  22.9 us
    unnamed x1, local copies, waits for them, and re-layouts  2.3 us

profile of v1, /device:TPU:24, one launch (start us, length us, event | category | flops | bytes accessed | tf_op | source)
XLA Modules:
  0.0 25.2 jit_solution(13736054064454691092)
XLA Ops:
  0.0 22.9 %shard_map.64 = bf16[256,2048]{1,0:T(8,128)(2,1)} custom-call(bf16[256,2048]{1,0:T(8,128)(2,1)} %q_hbm.1, bf16[256,256]{1,0:T(8,128)(2,1)} %k_hbm.1, bf16[256,256]{1,0:T(8,128)(2,1)} %v_hbm.1, s32[1,256]{1,0:T(1,128)} %bitcast.1, f32[2,256,128]{2,1,0:T(8,128)} %constant.4.clone.local_hbm, f32[4,2,128]{2,1,0:T(2,128)} %constant.5.clone.base_ref), custom_call_target="tpu_custom_call" | custom-call | tf_op jit(solution)/shard_map/pallas_call | solution.py:191
  22.9 2.3 %copy.8 = bf16[256,2048]{1,0:T(8,128)(2,1)} copy(bf16[256,2048]{1,0:T(8,128)(2,1)} %shard_map.64) | data formatting | bytes 2097152

commit v2 on v1

v2 whole, which is shorter than its diff:
```python
import functools
import math

import jax
import jax.numpy as jnp
import numpy as np
from jax import lax
from jax.experimental import pallas as pl
from jax.experimental.pallas import tpu as pltpu
from jax.sharding import PartitionSpec as P

HEAD_DIM = 128
ROPE_BASE = 500000.0
HIDDEN = -1e30
MESH = pl.DeviceIdType.MESH


def tables(rows, blocks):
    half = HEAD_DIM // 2
    freq = ROPE_BASE ** (-np.arange(half, dtype=np.float64) * 2.0 / HEAD_DIM)
    sign = np.concatenate([-np.ones(half), np.ones(half)])

    def pair(positions):
        angle = np.tile(positions[:, None] * freq[None, :], (1, 2))
        return np.cos(angle), np.sin(angle) * sign

    local = np.stack(pair(np.arange(rows, dtype=np.float64)))
    base = np.stack(pair(np.arange(blocks, dtype=np.float64) * rows), axis=1)
    return local.astype(np.float32), base.astype(np.float32)


def attend(
    n, chunks, q_hbm, k_hbm, v_hbm, id_hbm, local_hbm, base_hbm, out_ref,
    q_raw, q_turned, k_buf, v_buf, id_buf, local, base_ref, id_column, bias, acc, top, total,
    q_sem, own_sem, send_sem, recv_sem,
):
    me = lax.axis_index("cp")
    rows = q_hbm.shape[0]
    heads = q_hbm.shape[1] // HEAD_DIM
    kv_heads = k_hbm.shape[1] // HEAD_DIM
    group = heads // kv_heads
    chunk = rows // chunks
    right = jnp.minimum(me + 1, n - 1)
    left = jnp.maximum(me - 1, 0)

    barrier = pltpu.get_barrier_semaphore()

    @pl.when(me > 0)
    def _():
        pl.semaphore_signal(barrier, inc=1, device_id={"cp": left}, device_id_type=MESH)

    def span(c):
        return pl.ds(pl.multiple_of(c * chunk, chunk), chunk)

    def key_part(slot, c):
        return k_buf.at[slot, span(c), :]

    def value_part(slot, c):
        return v_buf.at[slot, span(c), :]

    own_copies = [
        pltpu.make_async_copy(id_hbm, id_buf.at[0], own_sem.at[0]),
        pltpu.make_async_copy(k_hbm, k_buf.at[0], own_sem.at[1]),
        pltpu.make_async_copy(v_hbm, v_buf.at[0], own_sem.at[2]),
    ]

    def remote(piece, source, target, slot):
        return pltpu.make_async_remote_copy(
            src_ref=source,
            dst_ref=target,
            send_sem=send_sem.at[slot, piece],
            recv_sem=recv_sem.at[slot, piece],
            device_id={"cp": right},
            device_id_type=MESH,
        )

    def id_hop(slot):
        return remote(0, id_buf.at[slot], id_buf.at[slot + 1], slot)

    def key_hop(slot, c):
        return remote(1 + 2 * c, key_part(slot, c), key_part(slot + 1, c), slot)

    def value_hop(slot, c):
        return remote(2 + 2 * c, value_part(slot, c), value_part(slot + 1, c), slot)

    def send(slot, c):
        @pl.when(c == 0)
        def _():
            id_hop(slot).start()

        key_hop(slot, c).start()
        value_hop(slot, c).start()

    q_copies = [pltpu.make_async_copy(q_hbm, q_raw, q_sem.at[0]),
                pltpu.make_async_copy(local_hbm, local, q_sem.at[1]),
                pltpu.make_async_copy(base_hbm, base_ref, q_sem.at[2])]
    for copy in own_copies + q_copies:
        copy.start()
    for copy in own_copies:
        copy.wait()

    @pl.when(me < n - 1)
    def _():
        pl.semaphore_wait(barrier, 1)
        for c in range(chunks):
            send(0, c)

    def phases(block, start, size):
        row = base_ref[block]
        cb, sb = row[0:1, :], row[1:2, :]
        cr = local[0, pl.ds(start, size), :]
        sr = local[1, pl.ds(start, size), :]
        return cb * cr - sb * sr, sb * cr + cb * sr

    def turn(x, cosine, sine):
        x = x.astype(jnp.float32)
        return x * cosine + pltpu.roll(x, HEAD_DIM // 2, axis=1) * sine

    for copy in q_copies:
        copy.wait()
    cosine, sine = phases(me, 0, rows)
    scale = math.log2(math.e) / math.sqrt(HEAD_DIM)
    cosine, sine = cosine * scale, sine * scale
    for h in range(heads):
        x = turn(q_raw[:, h * HEAD_DIM:(h + 1) * HEAD_DIM], cosine, sine)
        q_turned[h] = x.T.astype(jnp.bfloat16)
    acc[...] = jnp.zeros_like(acc)
    total[...] = jnp.zeros_like(total)
    top[...] = jnp.full_like(top, HIDDEN)
    row_index = lax.broadcasted_iota(jnp.int32, (chunk, rows), 1)
    key_index = lax.broadcasted_iota(jnp.int32, (chunk, rows), 0)

    def step(t, unused):
        k, c = t // chunks, t % chunks

        @pl.when(k > 0)
        def _():
            @pl.when(c == 0)
            def _():
                id_hop(k - 1).wait_recv()

            key_hop(k - 1, c).wait_recv()
            value_hop(k - 1, c).wait_recv()

            @pl.when(me < n - 1)
            def _():
                send(k, c)

        @pl.when(c == 0)
        def _():
            key_id = id_buf[k].astype(jnp.float32)
            id_column[...] = jnp.broadcast_to(key_id, (HEAD_DIM, rows)).T

        row_id = id_buf[0].astype(jnp.float32)
        key_id = id_column[span(c), :][:, :1]
        keep = (key_id == row_id) & (key_index + (c * chunk - k * rows) <= row_index)
        bias[...] = jnp.where(keep, 0.0, HIDDEN)
        cosine, sine = phases(me - k, pl.multiple_of(c * chunk, chunk), chunk)
        for g in range(kv_heads):
            lanes = slice(g * HEAD_DIM, (g + 1) * HEAD_DIM)
            key = turn(k_buf[k, span(c), lanes], cosine, sine).astype(jnp.bfloat16)
            value = v_buf[k, span(c), lanes].T
            for h in range(g * group, (g + 1) * group):
                scores = jnp.dot(key, q_turned[h], preferred_element_type=jnp.float32)
                scores = scores + bias[...]
                old = top[h:h + 1, :]
                new = jnp.maximum(old, jnp.max(scores, axis=0, keepdims=True))
                weights = jnp.exp2(scores - new)
                factor = jnp.exp2(old - new)
                top[h:h + 1, :] = new
                total[h:h + 1, :] = total[h:h + 1, :] * factor + jnp.sum(
                    weights, axis=0, keepdims=True
                )
                acc[h] = acc[h] * factor + jnp.dot(
                    value, weights.astype(jnp.bfloat16), preferred_element_type=jnp.float32
                )
        return unused

    lax.fori_loop(0, (me + 1) * chunks, step, 0)

    for h in range(heads):
        result = acc[h] * (1.0 / total[h:h + 1, :])
        out_ref[:, h * HEAD_DIM:(h + 1) * HEAD_DIM] = result.T.astype(out_ref.dtype)

    @pl.when(me < n - 1)
    def _():
        def drain(k, unused):
            id_hop(k).wait_send()
            for c in range(chunks):
                key_hop(k, c).wait_send()
                value_hop(k, c).wait_send()
            return unused

        lax.fori_loop(0, me + 1, drain, 0)


def body(n, queries, keys, values, segment_ids):
    rows, width = queries.shape
    kv_width = keys.shape[1]
    heads = width // HEAD_DIM
    chunks = 2
    chunk = rows // chunks
    local, base = tables(rows, n)
    anywhere = pl.BlockSpec(memory_space=pl.ANY)
    vmem = pl.BlockSpec(memory_space=pltpu.VMEM)
    count = 1 + 2 * chunks
    return pl.pallas_call(
        functools.partial(attend, n, chunks),
        out_shape=pltpu.VMEM((rows, width), queries.dtype),
        in_specs=[anywhere] * 6,
        out_specs=vmem,
        scratch_shapes=[
            pltpu.VMEM((rows, width), queries.dtype),
            pltpu.VMEM((heads, HEAD_DIM, rows), jnp.bfloat16),
            pltpu.VMEM((n, rows, kv_width), keys.dtype),
            pltpu.VMEM((n, rows, kv_width), values.dtype),
            pltpu.VMEM((n, 1, rows), jnp.int32),
            pltpu.VMEM((2, rows, HEAD_DIM), jnp.float32),
            pltpu.VMEM((n, 2, HEAD_DIM), jnp.float32),
            pltpu.VMEM((rows, HEAD_DIM), jnp.float32),
            pltpu.VMEM((chunk, rows), jnp.float32),
            pltpu.VMEM((heads, HEAD_DIM, rows), jnp.float32),
            pltpu.VMEM((heads, rows), jnp.float32),
            pltpu.VMEM((heads, rows), jnp.float32),
            pltpu.SemaphoreType.DMA((3,)),
            pltpu.SemaphoreType.DMA((3,)),
            pltpu.SemaphoreType.DMA((max(n - 1, 1), count)),
            pltpu.SemaphoreType.DMA((max(n - 1, 1), count)),
        ],
        compiler_params=pltpu.CompilerParams(collective_id=0, has_side_effects=True),
    )(queries, keys, values, segment_ids.reshape(1, rows), jnp.asarray(local), jnp.asarray(base))


def solution(mesh):
    return jax.shard_map(
        functools.partial(body, mesh.shape["cp"]),
        mesh=mesh,
        in_specs=(
            P(("rep", "cp"), "tp"),
            P(("rep", "cp"), "tp"),
            P(("rep", "cp"), "tp"),
            P(("rep", "cp")),
        ),
        out_specs=P(("rep", "cp"), "tp"),
        check_vma=False,
    )
```

time: 25.4 us -> 22.2 us (0.87)
  Pallas kernels: 22.9 us -> 21.1 us
  local copies, waits for them, and re-layouts: 2.3 us -> 0.97 us
    pallas_call x1, Pallas kernels: 22.9 us -> 21.1 us  [body(): pl.pallas_call(functools.partial(attend, n, chunks), out_shape=pltpu.VMEM...]
    unnamed x1, local copies, waits for them, and re-layouts: 2.3 us -> 0.97 us
where the time goes in v2:
time: 22.2 us; the launch traced here: 22.1 us
  Pallas kernels  21.1 us (95%)
  local copies, waits for them, and re-layouts  0.97 us (4%)
    pallas_call x1, Pallas kernels, body(): pl.pallas_call(functools.partial(attend, n, chunks), out_shape=pltpu.VMEM...  21.1 us
    unnamed x1, local copies, waits for them, and re-layouts  0.97 us

profile of v2, /device:TPU:24, one launch (start us, length us, event | category | flops | bytes accessed | tf_op | source)
XLA Modules:
  0.0 22.1 jit_solution(8831265871995821175)
XLA Ops:
  0.0 21.1 %shard_map.64 = bf16[256,2048]{1,0:T(8,128)(2,1)S(1)} custom-call(bf16[256,2048]{1,0:T(8,128)(2,1)} %q_hbm.1, bf16[256,256]{1,0:T(8,128)(2,1)} %k_hbm.1, bf16[256,256]{1,0:T(8,128)(2,1)} %v_hbm.1, s32[1,256]{1,0:T(1,128)} %bitcast.1, f32[2,256,128]{2,1,0:T(8,128)} %constant.4.clone.local_hbm, f32[4,2,128]{2,1,0:T(2,128)} %constant.5.clone.base_hbm), custom_call_target="tpu_custom_call" | custom-call | tf_op jit(solution)/shard_map/pallas_call | solution.py:207
  21.1 1.0 %copy.8 = bf16[256,2048]{1,0:T(8,128)(2,1)} copy(bf16[256,2048]{1,0:T(8,128)(2,1)S(1)} %shard_map.64) | data formatting | bytes 2097152

commit v3 on v2

--- a/solution.py
+++ b/solution.py
@@ -31,7 +31,7 @@
 
 def attend(
     n, chunks, q_hbm, k_hbm, v_hbm, id_hbm, local_hbm, base_hbm, out_ref,
-    q_raw, q_turned, k_buf, v_buf, id_buf, local, base_ref, id_column, bias, acc, top, total,
+    q_raw, q_turned, k_buf, v_buf, id_buf, local, base_ref, id_column, bias, weights, factor, acc, top, total,
     q_sem, own_sem, send_sem, recv_sem,
 ):
     me = lax.axis_index("cp")
@@ -83,14 +83,6 @@
     def value_hop(slot, c):
         return remote(2 + 2 * c, value_part(slot, c), value_part(slot + 1, c), slot)
 
-    def send(slot, c):
-        @pl.when(c == 0)
-        def _():
-            id_hop(slot).start()
-
-        key_hop(slot, c).start()
-        value_hop(slot, c).start()
-
     q_copies = [pltpu.make_async_copy(q_hbm, q_raw, q_sem.at[0]),
                 pltpu.make_async_copy(local_hbm, local, q_sem.at[1]),
                 pltpu.make_async_copy(base_hbm, base_ref, q_sem.at[2])]
@@ -102,8 +94,11 @@
     @pl.when(me < n - 1)
     def _():
         pl.semaphore_wait(barrier, 1)
+        id_hop(0).start()
         for c in range(chunks):
-            send(0, c)
+            key_hop(0, c).start()
+        for c in range(chunks):
+            value_hop(0, c).start()
 
     def phases(block, start, size):
         row = base_ref[block]
@@ -130,9 +125,7 @@
     row_index = lax.broadcasted_iota(jnp.int32, (chunk, rows), 1)
     key_index = lax.broadcasted_iota(jnp.int32, (chunk, rows), 0)
 
-    def step(t, unused):
-        k, c = t // chunks, t % chunks
-
+    def weigh(k, c):
         @pl.when(k > 0)
         def _():
             @pl.when(c == 0)
@@ -140,11 +133,14 @@
                 id_hop(k - 1).wait_recv()
 
             key_hop(k - 1, c).wait_recv()
-            value_hop(k - 1, c).wait_recv()
 
             @pl.when(me < n - 1)
             def _():
-                send(k, c)
+                @pl.when(c == 0)
+                def _():
+                    id_hop(k).start()
+
+                key_hop(k, c).start()
 
         @pl.when(c == 0)
         def _():
@@ -159,28 +155,59 @@
         for g in range(kv_heads):
             lanes = slice(g * HEAD_DIM, (g + 1) * HEAD_DIM)
             key = turn(k_buf[k, span(c), lanes], cosine, sine).astype(jnp.bfloat16)
-            value = v_buf[k, span(c), lanes].T
             for h in range(g * group, (g + 1) * group):
                 scores = jnp.dot(key, q_turned[h], preferred_element_type=jnp.float32)
                 scores = scores + bias[...]
                 old = top[h:h + 1, :]
                 new = jnp.maximum(old, jnp.max(scores, axis=0, keepdims=True))
-                weights = jnp.exp2(scores - new)
-                factor = jnp.exp2(old - new)
+                weight = jnp.exp2(scores - new)
+                change = jnp.exp2(old - new)
                 top[h:h + 1, :] = new
-                total[h:h + 1, :] = total[h:h + 1, :] * factor + jnp.sum(
-                    weights, axis=0, keepdims=True
+                factor[c, h:h + 1, :] = change
+                total[h:h + 1, :] = total[h:h + 1, :] * change + jnp.sum(
+                    weight, axis=0, keepdims=True
                 )
-                acc[h] = acc[h] * factor + jnp.dot(
-                    value, weights.astype(jnp.bfloat16), preferred_element_type=jnp.float32
-                )
+                weights[c, h] = weight.astype(jnp.bfloat16)
+
+    def gather(k, c, store):
+        @pl.when(k > 0)
+        def _():
+            value_hop(k - 1, c).wait_recv()
+
+            @pl.when(me < n - 1)
+            def _():
+                value_hop(k, c).start()
+
+        for g in range(kv_heads):
+            lanes = slice(g * HEAD_DIM, (g + 1) * HEAD_DIM)
+            value = v_buf[k, span(c), lanes].T
+            for h in range(g * group, (g + 1) * group):
+                store(h, acc[h] * factor[c, h:h + 1, :] + jnp.dot(
+                    value, weights[c, h], preferred_element_type=jnp.float32
+                ))
+
+    def keep_sum(h, result):
+        acc[h] = result
+
+    def finish(h, result):
+        result = result * (1.0 / total[h:h + 1, :])
+        out_ref[:, h * HEAD_DIM:(h + 1) * HEAD_DIM] = result.T.astype(out_ref.dtype)
+
+    def step(t, unused):
+        k, c = t // (2 * chunks), t % (2 * chunks)
+
+        @pl.when(c < chunks)
+        def _():
+            weigh(k, c)
+
+        @pl.when(c >= chunks)
+        def _():
+            gather(k, c - chunks, keep_sum)
+
         return unused
 
-    lax.fori_loop(0, (me + 1) * chunks, step, 0)
-
-    for h in range(heads):
-        result = acc[h] * (1.0 / total[h:h + 1, :])
-        out_ref[:, h * HEAD_DIM:(h + 1) * HEAD_DIM] = result.T.astype(out_ref.dtype)
+    lax.fori_loop(0, (me + 1) * 2 * chunks - 1, step, 0)
+    gather(me, chunks - 1, finish)
 
     @pl.when(me < n - 1)
     def _():
@@ -219,6 +246,8 @@
             pltpu.VMEM((n, 2, HEAD_DIM), jnp.float32),
             pltpu.VMEM((rows, HEAD_DIM), jnp.float32),
             pltpu.VMEM((chunk, rows), jnp.float32),
+            pltpu.VMEM((chunks, heads, chunk, rows), jnp.bfloat16),
+            pltpu.VMEM((chunks, heads, rows), jnp.float32),
             pltpu.VMEM((heads, HEAD_DIM, rows), jnp.float32),
             pltpu.VMEM((heads, rows), jnp.float32),
             pltpu.VMEM((heads, rows), jnp.float32),

time: 22.2 us -> 21.5 us (0.968)
  Pallas kernels: 21.1 us -> 20.4 us
    pallas_call x1, Pallas kernels: 21.1 us -> 20.4 us  [body(): pl.pallas_call(functools.partial(attend, n, chunks), out_shape=pltpu.VMEM...]
where the time goes in v3:
time: 21.5 us; the launch traced here: 21.4 us
  Pallas kernels  20.4 us (95%)
  local copies, waits for them, and re-layouts  0.97 us (5%)
    pallas_call x1, Pallas kernels, body(): pl.pallas_call(functools.partial(attend, n, chunks), out_shape=pltpu.VMEM...  20.4 us
    unnamed x1, local copies, waits for them, and re-layouts  0.97 us

profile of v3, /device:TPU:24, one launch (start us, length us, event | category | flops | bytes accessed | tf_op | source)
XLA Modules:
  0.0 21.4 jit_solution(1174341966378246402)
XLA Ops:
  0.0 20.4 %shard_map.64 = bf16[256,2048]{1,0:T(8,128)(2,1)S(1)} custom-call(bf16[256,2048]{1,0:T(8,128)(2,1)} %q_hbm.1, bf16[256,256]{1,0:T(8,128)(2,1)} %k_hbm.1, bf16[256,256]{1,0:T(8,128)(2,1)} %v_hbm.1, s32[1,256]{1,0:T(1,128)} %bitcast.1, f32[2,256,128]{2,1,0:T(8,128)} %constant.4.clone.local_hbm, f32[4,2,128]{2,1,0:T(2,128)} %constant.5.clone.base_hbm), custom_call_target="tpu_custom_call" | custom-call | tf_op jit(solution)/shard_map/pallas_call | solution.py:234
  20.4 1.0 %copy.8 = bf16[256,2048]{1,0:T(8,128)(2,1)} copy(bf16[256,2048]{1,0:T(8,128)(2,1)S(1)} %shard_map.64) | data formatting | bytes 2097152

commit v4 on v3

--- a/solution.py
+++ b/solution.py
@@ -12,6 +12,8 @@
 HEAD_DIM = 128
 ROPE_BASE = 500000.0
 HIDDEN = -1e30
+BURST = 4
+VMEM_LIMIT = 32 << 20
 MESH = pl.DeviceIdType.MESH
 
 
@@ -30,8 +32,9 @@
 
 
 def attend(
-    n, chunks, q_hbm, k_hbm, v_hbm, id_hbm, local_hbm, base_hbm, out_ref,
-    q_raw, q_turned, k_buf, v_buf, id_buf, local, base_ref, id_column, bias, weights, factor, acc, top, total,
+    n, chunks, q_hbm, k_hbm, v_hbm, id_hbm, local_hbm, base_hbm,
+    acc, weights, factor, total, v_last,
+    q_raw, q_turned, k_buf, v_buf, id_buf, local, base_ref, id_column, bias, top,
     q_sem, own_sem, send_sem, recv_sem,
 ):
     me = lax.axis_index("cp")
@@ -169,7 +172,7 @@
                 )
                 weights[c, h] = weight.astype(jnp.bfloat16)
 
-    def gather(k, c, store):
+    def arrive(k, c):
         @pl.when(k > 0)
         def _():
             value_hop(k - 1, c).wait_recv()
@@ -178,20 +181,15 @@
             def _():
                 value_hop(k, c).start()
 
+    def gather(k, c):
+        arrive(k, c)
         for g in range(kv_heads):
             lanes = slice(g * HEAD_DIM, (g + 1) * HEAD_DIM)
             value = v_buf[k, span(c), lanes].T
             for h in range(g * group, (g + 1) * group):
-                store(h, acc[h] * factor[c, h:h + 1, :] + jnp.dot(
+                acc[h] = acc[h] * factor[c, h:h + 1, :] + jnp.dot(
                     value, weights[c, h], preferred_element_type=jnp.float32
-                ))
-
-    def keep_sum(h, result):
-        acc[h] = result
-
-    def finish(h, result):
-        result = result * (1.0 / total[h:h + 1, :])
-        out_ref[:, h * HEAD_DIM:(h + 1) * HEAD_DIM] = result.T.astype(out_ref.dtype)
+                )
 
     def step(t, unused):
         k, c = t // (2 * chunks), t % (2 * chunks)
@@ -202,12 +200,13 @@
 
         @pl.when(c >= chunks)
         def _():
-            gather(k, c - chunks, keep_sum)
+            gather(k, c - chunks)
 
         return unused
 
     lax.fori_loop(0, (me + 1) * 2 * chunks - 1, step, 0)
-    gather(me, chunks - 1, finish)
+    arrive(me, chunks - 1)
+    v_last[...] = v_buf[me, span(chunks - 1), :]
 
     @pl.when(me < n - 1)
     def _():
@@ -221,6 +220,31 @@
         lax.fori_loop(0, me + 1, drain, 0)
 
 
+def finish(acc, weights, factor, total, v_last, out_hbm, stage, sem):
+    last, heads = weights.shape[0] - 1, acc.shape[0]
+    kv_heads = v_last.shape[1] // HEAD_DIM
+    group = heads // kv_heads
+    burst = math.gcd(group, BURST)
+    copies = []
+    for h in range(heads):
+        g = h // group
+        if h % group == 0:
+            value = v_last[:, g * HEAD_DIM:(g + 1) * HEAD_DIM].T
+        result = acc[h] * factor[last, h:h + 1, :] + jnp.dot(
+            value, weights[last, h], preferred_element_type=jnp.float32
+        )
+        result = result * (1.0 / total[h:h + 1, :])
+        stage[:, h * HEAD_DIM:(h + 1) * HEAD_DIM] = result.T.astype(stage.dtype)
+        if (h + 1) % burst == 0:
+            lanes = pl.ds((h + 1 - burst) * HEAD_DIM, burst * HEAD_DIM)
+            copies.append(pltpu.make_async_copy(
+                stage.at[:, lanes], out_hbm.at[:, lanes], sem.at[len(copies)]
+            ))
+            copies[-1].start()
+    for copy in copies:
+        copy.wait()
+
+
 def body(n, queries, keys, values, segment_ids):
     rows, width = queries.shape
     kv_width = keys.shape[1]
@@ -228,14 +252,22 @@
     chunks = 2
     chunk = rows // chunks
     local, base = tables(rows, n)
-    anywhere = pl.BlockSpec(memory_space=pl.ANY)
+    anywhere = pl.BlockSpec(memory_space=pltpu.HBM)
     vmem = pl.BlockSpec(memory_space=pltpu.VMEM)
     count = 1 + 2 * chunks
-    return pl.pallas_call(
+    operands = (queries, keys, values, segment_ids.reshape(1, rows),
+                jnp.asarray(local), jnp.asarray(base))
+    state = pl.pallas_call(
         functools.partial(attend, n, chunks),
-        out_shape=pltpu.VMEM((rows, width), queries.dtype),
+        out_shape=[
+            pltpu.VMEM((heads, HEAD_DIM, rows), jnp.float32),
+            pltpu.VMEM((chunks, heads, chunk, rows), jnp.bfloat16),
+            pltpu.VMEM((chunks, heads, rows), jnp.float32),
+            pltpu.VMEM((heads, rows), jnp.float32),
+            pltpu.VMEM((chunk, kv_width), values.dtype),
+        ],
         in_specs=[anywhere] * 6,
-        out_specs=vmem,
+        out_specs=[vmem] * 5,
         scratch_shapes=[
             pltpu.VMEM((rows, width), queries.dtype),
             pltpu.VMEM((heads, HEAD_DIM, rows), jnp.bfloat16),
@@ -246,18 +278,27 @@
             pltpu.VMEM((n, 2, HEAD_DIM), jnp.float32),
             pltpu.VMEM((rows, HEAD_DIM), jnp.float32),
             pltpu.VMEM((chunk, rows), jnp.float32),
-            pltpu.VMEM((chunks, heads, chunk, rows), jnp.bfloat16),
-            pltpu.VMEM((chunks, heads, rows), jnp.float32),
-            pltpu.VMEM((heads, HEAD_DIM, rows), jnp.float32),
-            pltpu.VMEM((heads, rows), jnp.float32),
             pltpu.VMEM((heads, rows), jnp.float32),
             pltpu.SemaphoreType.DMA((3,)),
             pltpu.SemaphoreType.DMA((3,)),
             pltpu.SemaphoreType.DMA((max(n - 1, 1), count)),
             pltpu.SemaphoreType.DMA((max(n - 1, 1), count)),
         ],
-        compiler_params=pltpu.CompilerParams(collective_id=0, has_side_effects=True),
-    )(queries, keys, values, segment_ids.reshape(1, rows), jnp.asarray(local), jnp.asarray(base))
+        compiler_params=pltpu.CompilerParams(
+            collective_id=0, has_side_effects=True, vmem_limit_bytes=VMEM_LIMIT
+        ),
+    )(*[pltpu.with_memory_space_constraint(x, pltpu.HBM) for x in operands])
+    return pl.pallas_call(
+        finish,
+        out_shape=jax.ShapeDtypeStruct((rows, width), queries.dtype),
+        in_specs=[vmem] * 5,
+        out_specs=anywhere,
+        scratch_shapes=[
+            pltpu.VMEM((rows, width), queries.dtype),
+            pltpu.SemaphoreType.DMA((heads,)),
+        ],
+        compiler_params=pltpu.CompilerParams(vmem_limit_bytes=VMEM_LIMIT),
+    )(*state)
 
 
 def solution(mesh):

time: 21.5 us -> 21.4 us (level)
  local copies, waits for them, and re-layouts: 0.97 us -> 0 us
  Pallas kernels: 20.4 us -> 21.2 us
    unnamed x1 -> x0, local copies, waits for them, and re-layouts: 0.97 us -> none
    pallas_call x1 -> x2, Pallas kernels: 20.4 us -> 21.2 us  [the longest x1 19.7 us: body(): pl.pallas_call(functools.partial(attend, n, chunks), out_shape=[pltpu.VME...]
where the time goes in v4:
time: 21.4 us; the launch traced here: 21.2 us
  Pallas kernels  21.2 us (99%)
    pallas_call x1, Pallas kernels, body(): pl.pallas_call(functools.partial(attend, n, chunks), out_shape=[pltpu.VME...  19.7 us
    pallas_call x1, Pallas kernels, body(): pl.pallas_call(finish, out_shape=jax.ShapeDtypeStruct((rows, width), quer...  1.49 us

profile of v4, /device:TPU:24, one launch (start us, length us, event | category | flops | bytes accessed | tf_op | source)
XLA Modules:
  0.0 21.2 jit_solution(7299637364145767647)
XLA Ops:
  0.0 19.7 %shard_map.64 = (f32[16,128,256]{2,1,0:T(8,128)S(1)}, bf16[2,16,128,256]{3,2,1,0:T(8,128)(2,1)S(1)}, f32[2,16,256]{2,1,0:T(8,128)S(1)}, f32[16,256]{1,0:T(8,128)S(1)}, bf16[128,256]{1,0:T(8,128)(2,1)S(1)}) custom-call(bf16[256,2048]{1,0:T(8,128)(2,1)} %q_hbm.1, bf16[256,256]{1,0:T(8,128)(2,1)} %k_hbm.1, bf16[256,256]{1,0:T(8,128)(2,1)} %v_hbm.1, ...), custom_call_target="tpu_custom_call" | custom-call | tf_op jit(solution)/shard_map/pallas_call | solution.py:260
  19.7 1.5 %shard_map.65 = bf16[256,2048]{1,0:T(8,128)(2,1)} custom-call(f32[16,128,256]{2,1,0:T(8,128)S(1)} %get-tuple-element.10.acc, bf16[2,16,128,256]{3,2,1,0:T(8,128)(2,1)S(1)} %get-tuple-element.11.weights, f32[2,16,256]{2,1,0:T(8,128)S(1)} %get-tuple-element.12.factor, f32[16,256]{1,0:T(8,128)S(1)} %get-tuple-element.13.total, ...), custom_call_target="tpu_custom_call" | custom-call | tf_op jit(solution)/shard_map/pallas_call | solution.py:291
